TPU v7x, 32 devices: a whole 2x2x4 slice. The times are simulated.
32 devices in a mesh: dp: 8 (over z, core), expert: 4 (over y, x).
Axes of the slice: x: 2, y: 2, z: 4, core: 2. Of those that a mesh axis runs over, the one named last changes fastest.
Arguments:
- tokens: bfloat16 [4096, 2048], P(('dp', 'expert')), may hold values from -6 to 6
- expert_ids: int32 [4096, 8], P(('dp', 'expert')), may hold values from 0 to 127, as said below
- gate_probs: float32 [4096, 8], P(('dp', 'expert')), may hold values from 0.1 to 1
- cotangent: bfloat16 [4096, 2048], P(('dp', 'expert')), may hold values from -1.5 to 1.5
- expert_weights: bfloat16 [2048, 4, 3, 768], P(None, 'expert'), may hold values from -0.21875 to 0.21875
Outputs:
- mixed: bfloat16 [4096, 2048], P(('dp', 'expert'))
- grad_tokens: bfloat16 [4096, 2048], P(('dp', 'expert'))
- grad_gates: float32 [4096, 8], P(('dp', 'expert'))
- grad_weights: bfloat16 [2048, 4, 3, 768], P('dp', 'expert')
Inputs may be any that keep to these rules, and one draw needn't show every extreme that they name: `expert_ids`: each row names 8 different experts. In the rows of one device every expert below 4 is named by 1 to 24 rows, and for every index of dp some such expert is named by exactly 24 rows of each device of that index.
All inputs are finite; a program needn't handle non-finite values.
Results may differ from a plain program's by a relative error of at most 0.0058.
Values may be sent and summed in bfloat16 or wider, within the bound.
No kernel may reach another device: no remote copies, remote signals or barrier semaphores. Data moves between devices by JAX's collectives and lax.ppermute only.
A program may use at most 128 MiB of HBM per device.

v0:
```python
import jax
import jax.numpy as jnp
from jax import lax
from jax.sharding import PartitionSpec as P

BLOCK = 128
CAP = 24


def expert_rows(x_rows, dy_rows, weights):
    w_gate = weights[:, 0, :]
    w_up = weights[:, 1, :]
    w_down = weights[:, 2, :]
    contract_last = (((1,), (1,)), ((), ()))
    gate_proj = jnp.dot(x_rows, w_gate, preferred_element_type=jnp.float32)
    up_proj = jnp.dot(x_rows, w_up, preferred_element_type=jnp.float32)
    sigmoid_gate = jax.nn.sigmoid(gate_proj)
    silu_gate = gate_proj * sigmoid_gate
    hidden = (silu_gate * up_proj).astype(jnp.bfloat16)
    expert_out = lax.dot_general(
        hidden, w_down, contract_last, preferred_element_type=jnp.float32
    ).astype(jnp.bfloat16)
    hidden_grad = jnp.dot(dy_rows, w_down, preferred_element_type=jnp.float32)
    gate_grad = (
        hidden_grad * up_proj * sigmoid_gate * (1.0 + gate_proj * (1.0 - sigmoid_gate))
    ).astype(jnp.bfloat16)
    up_grad = (hidden_grad * silu_gate).astype(jnp.bfloat16)
    token_part = (
        lax.dot_general(gate_grad, w_gate, contract_last, preferred_element_type=jnp.float32)
        + lax.dot_general(up_grad, w_up, contract_last, preferred_element_type=jnp.float32)
    ).astype(jnp.bfloat16)
    return (expert_out, token_part, hidden, gate_grad, up_grad)


def squeeze_live(rows_x, rows_dy):
    total_rows = rows_x.shape[0]
    padded_rows = -(-total_rows // BLOCK) * BLOCK
    is_live = jnp.any(rows_x != 0, axis=1)
    live_count = is_live.astype(jnp.int32)
    live_total = jnp.sum(live_count)
    placement = jnp.where(
        is_live, jnp.cumsum(live_count) - 1, live_total + jnp.cumsum(1 - live_count) - 1
    )
    source_row = (
        jnp.zeros((padded_rows,), jnp.int32)
        .at[placement]
        .set(jnp.arange(total_rows, dtype=jnp.int32))
    )
    keep_row = (jnp.arange(padded_rows) < live_total)[:, None]
    packed_x = jnp.where(keep_row, rows_x[source_row], jnp.zeros((), rows_x.dtype))
    packed_dy = jnp.where(keep_row, rows_dy[source_row], jnp.zeros((), rows_dy.dtype))
    return (packed_x, packed_dy, placement, live_total)


def run_expert(rows_x, rows_dy, weights):
    packed_x, packed_dy, placement, live_total = squeeze_live(rows_x, rows_dy)
    padded_rows, model_width = packed_x.shape
    hidden_units = weights.shape[2]
    block_total = (live_total + BLOCK - 1) // BLOCK

    def block_step(block_index, state_in):
        row_start = block_index * BLOCK
        x_block = lax.dynamic_slice_in_dim(packed_x, row_start, BLOCK, 0)
        dy_block = lax.dynamic_slice_in_dim(packed_dy, row_start, BLOCK, 0)
        results = expert_rows(x_block, dy_block, weights)
        return tuple(
            (
                lax.dynamic_update_slice_in_dim(full_array, block_part, row_start, 0)
                for full_array, block_part in zip(state_in, results)
            )
        )

    initial = (
        jnp.zeros((padded_rows, model_width), jnp.bfloat16),
        jnp.zeros((padded_rows, model_width), jnp.bfloat16),
        jnp.zeros((padded_rows, hidden_units), jnp.bfloat16),
        jnp.zeros((padded_rows, hidden_units), jnp.bfloat16),
        jnp.zeros((padded_rows, hidden_units), jnp.bfloat16),
    )
    out_all, part_all, hidden_all, gate_all, up_all = lax.fori_loop(
        0, block_total, block_step, initial
    )
    contract_first = (((0,), (0,)), ((), ()))
    groups = lax.axis_size("dp")
    width_part = model_width // groups
    split_x = packed_x.reshape(padded_rows, groups, width_part)
    split_dy = packed_dy.reshape(padded_rows, groups, width_part)
    recv_x, recv_dy = (
        lax.all_to_all(split_x, "dp", split_axis=1, concat_axis=0, tiled=True),
        lax.all_to_all(split_dy, "dp", split_axis=1, concat_axis=0, tiled=True),
    )
    recv_x = recv_x.reshape(groups * padded_rows, width_part)
    recv_dy = recv_dy.reshape(groups * padded_rows, width_part)
    gate_piece = lax.all_gather(gate_all, "dp", axis=0, tiled=True)
    up_piece = lax.all_gather(up_all, "dp", axis=0, tiled=True)
    hidden_piece = lax.all_gather(hidden_all, "dp", axis=0, tiled=True)
    gate_term = lax.dot_general(
        recv_x, gate_piece, contract_first, preferred_element_type=jnp.float32
    )
    up_term = lax.dot_general(recv_x, up_piece, contract_first, preferred_element_type=jnp.float32)
    down_term = lax.dot_general(
        recv_dy, hidden_piece, contract_first, preferred_element_type=jnp.float32
    )
    folded = jnp.stack([gate_term, up_term, down_term], axis=1)
    summed = folded[:, None, :, :]
    return (out_all[placement], part_all[placement], summed)


def per_device(tokens, expert_ids, gate_probs, cotangent, expert_weights):
    tok_rows, model_width = tokens.shape
    top_count = expert_ids.shape[1]
    held_count = lax.axis_size("expert")
    slot_total = held_count * CAP
    flat_ids = expert_ids.reshape(-1)
    is_held = flat_ids < held_count
    onehot = (flat_ids[:, None] == jnp.arange(held_count, dtype=jnp.int32)[None, :]).astype(
        jnp.int32
    )
    position = jnp.sum(jnp.cumsum(onehot, axis=0) * onehot, axis=1) - 1
    destination = jnp.where(is_held, flat_ids * CAP + position, slot_total)
    source_token = jnp.arange(tok_rows * top_count, dtype=jnp.int32) // top_count
    slot_token = jnp.zeros((slot_total,), jnp.int32).at[destination].set(source_token, mode="drop")
    slot_prob = (
        jnp.zeros((slot_total,), jnp.float32)
        .at[destination]
        .set(gate_probs.reshape(-1), mode="drop")
    )
    slot_live = jnp.zeros((slot_total,), jnp.bool_).at[destination].set(True, mode="drop")
    send_x = jnp.where(slot_live[:, None], tokens[slot_token], jnp.zeros((), jnp.bfloat16))
    send_dy = (slot_prob[:, None] * cotangent[slot_token].astype(jnp.float32)).astype(jnp.bfloat16)
    recv_x, recv_dy = (
        lax.all_to_all(
            send_x.reshape(held_count, CAP, model_width),
            "expert",
            split_axis=0,
            concat_axis=0,
            tiled=True,
        ),
        lax.all_to_all(
            send_dy.reshape(held_count, CAP, model_width),
            "expert",
            split_axis=0,
            concat_axis=0,
            tiled=True,
        ),
    )
    rows_x = recv_x.reshape(slot_total, model_width)
    rows_dy = recv_dy.reshape(slot_total, model_width)
    weights = expert_weights[:, 0]
    out_rows, part_rows, summed = run_expert(rows_x, rows_dy, weights)
    back_out, back_part = (
        lax.all_to_all(
            out_rows.reshape(held_count, CAP, model_width),
            "expert",
            split_axis=0,
            concat_axis=0,
            tiled=True,
        ),
        lax.all_to_all(
            part_rows.reshape(held_count, CAP, model_width),
            "expert",
            split_axis=0,
            concat_axis=0,
            tiled=True,
        ),
    )
    safe_slot = jnp.where(is_held, destination, 0)
    took_out = jnp.where(
        is_held[:, None],
        back_out.reshape(slot_total, model_width)[safe_slot].astype(jnp.float32),
        jnp.zeros((), jnp.float32),
    ).reshape(tok_rows, top_count, model_width)
    took_part = jnp.where(
        is_held[:, None],
        back_part.reshape(slot_total, model_width)[safe_slot].astype(jnp.float32),
        jnp.zeros((), jnp.float32),
    ).reshape(tok_rows, top_count, model_width)
    mixed_out = jnp.sum(gate_probs[:, :, None] * took_out, axis=1).astype(jnp.bfloat16)
    grad_gates = jnp.sum(took_out * cotangent.astype(jnp.float32)[:, None, :], axis=2)
    grad_tokens = jnp.sum(took_part, axis=1).astype(jnp.bfloat16)
    return (mixed_out, grad_tokens, grad_gates, summed.astype(jnp.bfloat16))


def solution(mesh):
    in_specs = (
        P(("dp", "expert"), None),
        P(("dp", "expert"), None),
        P(("dp", "expert"), None),
        P(("dp", "expert"), None),
        P(None, "expert", None, None),
    )
    out_specs = (
        P(("dp", "expert"), None),
        P(("dp", "expert"), None),
        P(("dp", "expert"), None),
        P("dp", "expert", None, None),
    )
    return jax.shard_map(
        per_device, mesh=mesh, in_specs=in_specs, out_specs=out_specs, check_vma=False
    )
```

profile of v0, /device:TPU:0, one launch (start us, length us, event | category | flops | bytes accessed | tf_op | source)
XLA Modules:
  0.0 165.4 jit_solution(4226696876934039421)
XLA Ops:
  12.3 4.3 %scatter_custom_fusion.1 = s32[96]{0:T(128)S(1)} fusion(s32[1024]{0:T(1024)S(1)} %bitcast.105, s32[1024]{0:T(1024)S(1)} %add_select_fusion, s32[]{:T(128)} %copy.53), kind=kCustom, calls=%fused_computation.100 | custom fusion | bytes 388 | tf_op jit(solution)/shard_map/scatter | solution.py:122
  16.7 4.3 %scatter_custom_fusion = pred[96]{0:T(512)(128)(4,1)S(1)} fusion(s32[1024]{0:T(1024)S(1)} %bitcast.106, pred[1024]{0:T(1024)(128)(4,1)S(1)} %broadcast.259, pred[]{:T(512)} %constant.84.clone.1), kind=kCustom, calls=%fused_computation.92 | custom fusion | bytes 97 | tf_op jit(solution)/shard_map/scatter | solution.py:128
  22.8 5.2 %all-to-all-start = ((bf16[4,24,2048]{2,1,0:T(8,128)(2,1)}), bf16[4,24,2048]{2,1,0:T(8,128)(2,1)S(1)}, u32[]{:S(2)}, u32[]{:S(2)}) async-start(bf16[4,24,2048]{2,1,0:T(8,128)(2,1)} %broadcast_select_fusion.1), calls=%async_computation | async-start | bytes 786432 | tf_op jit(solution)/shard_map/all_to_all | solution.py:132
  29.1 4.3 %scatter_custom_fusion.3 = f32[96]{0:T(128)S(1)} fusion(s32[1024]{0:T(1024)S(1)} %bitcast.107, f32[1024]{0:T(1024)S(1)} %reshape.410, f32[]{:T(128)} %constant.94.clone.1), kind=kCustom, calls=%fused_computation.95 | custom fusion | bytes 388 | tf_op jit(solution)/shard_map/scatter | solution.py:126
  34.6 3.9 %all-to-all-start.1 = ((bf16[4,24,2048]{2,1,0:T(8,128)(2,1)}), bf16[4,24,2048]{2,1,0:T(8,128)(2,1)S(1)}, u32[]{:S(2)}, u32[]{:S(2)}) async-start(bf16[4,24,2048]{2,1,0:T(8,128)(2,1)} %fusion.18), calls=%async_computation.1 | async-start | bytes 786432 | tf_op jit(solution)/shard_map/all_to_all | solution.py:139
  44.2 2.7 %negate_exponential_fusion = (f32[128,768]{1,0:T(8,128)S(1)}, f32[128,768]{1,0:T(8,128)S(1)}) fusion(bf16[2048,3,768]{2,0,1:T(8,128)(2,1)} %bitcast.108, bf16[128,2048]{1,0:T(8,128)(2,1)S(1)} %gather_fusion.1, pred[128]{0:T(512)(128)(4,1)S(1)} %iota_compare_fusion.2), kind=kOutput, calls=%fused_computation.56 | convolution fusion | flops 403013632 | bytes 4456576 | tf_op jit(solution)/shard_map/while/body/dot_general | solution.py:15
  50.4 3.5 %fusion.46 = (f32[128,768]{1,0:T(8,128)S(1)}, f32[128,768]{1,0:T(8,128)}) fusion(f32[128,768]{1,0:T(8,128)S(1)} %fusion.9, bf16[2048,3,768]{2,0,1:T(8,128)(2,1)} %bitcast.110, bf16[128,2048]{1,0:T(8,128)(2,1)S(1)} %gather_fusion.3, pred[128]{0:T(512)(128)(4,1)S(1)} %iota_compare_fusion.2), kind=kOutput, calls=%fused_computation.108 | convolution fusion | flops 403013632 | bytes 4849792 | tf_op jit(solution)/shard_map/while/body/dot_general | solution.py:23
  53.9 3.2 %fusion.14 = bf16[128,2048]{1,0:T(8,128)(2,1)S(1)} fusion(bf16[2048,3,768]{2,0,1:T(8,128)(2,1)} %bitcast.111, f32[128,768]{1,0:T(8,128)S(1)} %fusion.9, f32[128,768]{1,0:T(8,128)S(1)} %get-tuple-element.446), kind=kOutput, calls=%fused_computation.36 | convolution fusion | flops 403505152 | bytes 4456448 | tf_op jit(solution)/shard_map/while/body/dot_general | solution.py:20
  57.1 4.0 %fusion.6 = f32[128,2048]{1,0:T(8,128)} fusion(bf16[2048,3,768]{2,0,1:T(8,128)(2,1)} %bitcast.112, f32[128,768]{1,0:T(8,128)S(1)} %get-tuple-element.446, f32[128,768]{1,0:T(8,128)S(1)} %get-tuple-element.448), kind=kOutput, calls=%fused_computation.28 | convolution fusion | flops 403537920 | bytes 4980736 | tf_op jit(solution)/shard_map/while/body/dot_general | solution.py:29
  61.1 3.4 %fusion.13 = bf16[128,2048]{1,0:T(8,128)(2,1)S(1)} fusion(f32[128,2048]{1,0:T(8,128)} %fusion.6, bf16[2048,3,768]{2,0,1:T(8,128)(2,1)} %bitcast.113, f32[128,768]{1,0:T(8,128)} %get-tuple-element.449, f32[128,768]{1,0:T(8,128)S(1)} %get-tuple-element.446), kind=kOutput, calls=%fused_computation.35 | convolution fusion | flops 403767296 | bytes 5505024 | tf_op jit(solution)/shard_map/while/body/dot_general | solution.py:30
  68.3 3.7 %while.24 = (s32[]{:T(128)}, bf16[128,2048]{1,0:T(8,128)(2,1)}, bf16[128,2048]{1,0:T(8,128)(2,1)}, bf16[128,768]{1,0:T(8,128)(2,1)}, bf16[128,768]{1,0:T(8,128)(...) while((s32[]{:T(128)}, bf16[128,2048]{1,0:T(8,128)(2,1)}, ...), condition=%wide.region_12.13_spmd, body=%wide.region_11.12_spmd.sunk | while | flops 1277954 | bytes 4653197 | solution.py:80
  72.8 3.2 %gather_fusion.4 = bf16[96,2048]{1,0:T(8,128)(2,1)} fusion(bf16[128,2048]{1,0:T(8,128)(2,1)} %get-tuple-element.306, s32[1024]{0:T(1024)S(1)} %pad_clamp_fusion), kind=kCustom, calls=%fused_computation.4 | custom fusion | bytes 786816 | tf_op jit(solution)/shard_map/gather | solution.py:106
  76.0 4.2 %all-to-all-start.2 = ((bf16[4,24,2048]{2,1,0:T(8,128)(2,1)}), bf16[4,24,2048]{2,1,0:T(8,128)(2,1)S(1)}, u32[]{:S(2)}, u32[]{:S(2)}) async-start(bf16[4,24,2048]{2,1,0:T(8,128)(2,1)} %bitcast.11), calls=%async_computation.2 | async-start | bytes 786432 | tf_op jit(solution)/shard_map/all_to_all | solution.py:152
  82.5 3.6 %all-to-all-done.2 = bf16[4,24,2048]{2,1,0:T(8,128)(2,1)S(1)} async-done(((bf16[4,24,2048]{2,1,0:T(8,128)(2,1)}), bf16[4,24,2048]{2,1,0:T(8,128)(2,1)S(1)}, u32[]{:S(2)}, u32[]{:S(2)}) %all-to-all-start.2) | async-done | bytes 393248 | tf_op jit(solution)/shard_map/all_to_all | solution.py:152
  86.0 3.5 %all-to-all-start.3 = ((bf16[4,24,2048]{2,1,0:T(8,128)(2,1)}), bf16[4,24,2048]{2,1,0:T(8,128)(2,1)S(1)}, u32[]{:S(2)}, u32[]{:S(2)}) async-start(bf16[4,24,2048]{2,1,0:T(8,128)(2,1)} %bitcast.15), calls=%async_computation.3 | async-start | bytes 786432 | tf_op jit(solution)/shard_map/all_to_all | solution.py:159
  90.7 4.7 %all-to-all-done.3 = bf16[4,24,2048]{2,1,0:T(8,128)(2,1)S(1)} async-done(((bf16[4,24,2048]{2,1,0:T(8,128)(2,1)}), bf16[4,24,2048]{2,1,0:T(8,128)(2,1)S(1)}, u32[]{:S(2)}, u32[]{:S(2)}) %all-to-all-start.3) | async-done | bytes 393248 | tf_op jit(solution)/shard_map/all_to_all | solution.py:159
  95.3 4.9 %all-to-all-start.4 = ((bf16[128,8,256]{2,0,1:T(8,128)(2,1)}), bf16[128,8,256]{2,0,1:T(8,128)(2,1)S(1)}, u32[]{:S(2)}, u32[]{:S(2)}) async-start(bf16[128,8,256]{2,0,1:T(8,128)(2,1)} %get-tuple-element.350), calls=%async_computation.4 | async-start | bytes 1048576 | tf_op jit(solution)/shard_map/all_to_all | solution.py:89
  100.5 6.0 %gather_fusion.5 = bf16[1024,2048]{1,0:T(8,128)(2,1)} fusion(bf16[96,2048]{1,0:T(8,128)(2,1)S(1)} %bitcast.91, s32[1024]{0:T(1024)S(1)} %broadcast_clamp_fusion), kind=kCustom, calls=%fused_computation.5 | custom fusion | bytes 8392704 | tf_op jit(solution)/shard_map/gather | solution.py:170
  106.5 6.0 %gather_fusion.7 = bf16[1024,2048]{1,0:T(8,128)(2,1)} fusion(bf16[96,2048]{1,0:T(8,128)(2,1)S(1)} %bitcast.92, s32[1024]{0:T(1024)S(1)} %broadcast_clamp_fusion), kind=kCustom, calls=%fused_computation.7 | custom fusion | bytes 8392704 | tf_op jit(solution)/shard_map/gather | solution.py:175
  112.5 3.3 %fusion.4 = f32[1024]{0:T(1024)S(1)} fusion(bf16[1024,2048]{1,0:T(8,128)(2,1)} %gather_fusion.5, f32[128,2048]{1,0:T(8,128)S(1)} %convert_element_type.142, pred[1024]{0:T(1024)(128)(4,1)S(1)} %broadcast_in_dim.103), kind=kLoop, calls=%fused_computation.22 | loop fusion | flops 8387584 | bytes 5248000 | tf_op jit(solution)/shard_map/reduce_sum | solution.py:179
  116.5 5.3 %all-to-all-done.4 = bf16[128,8,256]{2,0,1:T(8,128)(2,1)S(1)} async-done(((bf16[128,8,256]{2,0,1:T(8,128)(2,1)}), bf16[128,8,256]{2,0,1:T(8,128)(2,1)S(1)}, u32[]{:S(2)}, u32[]{:S(2)}) %all-to-all-start.4) | async-done | bytes 524320 | tf_op jit(solution)/shard_map/all_to_all | solution.py:89
  121.8 3.7 %all-to-all-start.5 = ((bf16[128,8,256]{2,0,1:T(8,128)(2,1)}), bf16[128,8,256]{2,0,1:T(8,128)(2,1)S(1)}, u32[]{:S(2)}, u32[]{:S(2)}) async-start(bf16[128,8,256]{2,0,1:T(8,128)(2,1)} %get-tuple-element.351), calls=%async_computation.5 | async-start | bytes 1048576 | tf_op jit(solution)/shard_map/all_to_all | solution.py:90
  125.6 10.4 %fusion.5 = (bf16[128,2048]{1,0:T(8,128)(2,1)}, bf16[128,2048]{1,0:T(8,128)(2,1)}) fusion(bf16[1024,2048]{1,0:T(8,128)(2,1)} %gather_fusion.7, pred[128,8]{1,0:T(8,128)(4,1)S(1)} %copy.15, bf16[1024,2048]{1,0:T(8,128)(2,1)} %gather_fusion.5, f32[128,8]{1,0:T(8,128)S(1)} %copy-done.9), kind=kLoop, calls=%fused_computation.24 | loop fusion | flops 14155776 | bytes 9442304 | tf_op jit(solution)/shard_map/reduce_sum | solution.py:180
  140.6 15.1 %all-gather.8.cloned.1.call-done = bf16[1024,768]{1,0:T(8,128)(2,1)} async-done(((bf16[128,768]{1,0:T(8,128)(2,1)}), bf16[1024,768]{1,0:T(8,128)(2,1)}) %all-gather.8.cloned.1.call-update) | async-done | bytes 1572880 | tf_op jit(solution)/shard_map/all_gather | solution.py:96
  (103 shorter events, 38.0 us)
Async XLA Ops:
  7.2 14.0 %copy-start = (bf16[128,2048]{1,0:T(8,128)(2,1)S(1)}, bf16[128,2048]{1,0:T(8,128)(2,1)}, u32[]{:S(2)}) copy-start(bf16[128,2048]{1,0:T(8,128)(2,1)} %param.7) | copy-start | bytes 1572868
  7.2 20.8 %copy-start.1 = (bf16[128,2048]{1,0:T(8,128)(2,1)S(1)}, bf16[128,2048]{1,0:T(8,128)(2,1)}, u32[]{:S(2)}) copy-start(bf16[128,2048]{1,0:T(8,128)(2,1)} %param.10) | copy-start | bytes 1572868
  21.1 7.7 %copy-start.11 = (f32[128,8]{0,1:T(8,128)S(1)}, f32[128,8]{0,1:T(8,128)}, u32[]{:S(2)}) copy-start(f32[128,8]{0,1:T(8,128)} %param.9) | copy-start | bytes 12292
  22.8 11.8 %all-to-all-start = ((bf16[4,24,2048]{2,1,0:T(8,128)(2,1)}), bf16[4,24,2048]{2,1,0:T(8,128)(2,1)S(1)}, u32[]{:S(2)}, u32[]{:S(2)}) async-start(bf16[4,24,2048]{2,1,0:T(8,128)(2,1)} %broadcast_select_fusion.1), calls=%async_computation | async-start | bytes 786432 | tf_op jit(solution)/shard_map/all_to_all | solution.py:132
  29.0 15.2 %copy-start.8 = (f32[128,8]{1,0:T(8,128)}, f32[128,8]{1,0:T(8,128)S(1)}, u32[]{:S(2)}) copy-start(f32[128,8]{1,0:T(8,128)S(1)} %copy.14) | copy-start | bytes 12292
  34.6 14.8 %all-to-all-start.1 = ((bf16[4,24,2048]{2,1,0:T(8,128)(2,1)}), bf16[4,24,2048]{2,1,0:T(8,128)(2,1)S(1)}, u32[]{:S(2)}, u32[]{:S(2)}) async-start(bf16[4,24,2048]{2,1,0:T(8,128)(2,1)} %fusion.18), calls=%async_computation.1 | async-start | bytes 786432 | tf_op jit(solution)/shard_map/all_to_all | solution.py:139
  38.5 97.5 %all-gather.4.cloned.1.call-start = ((), (), s32[]{:S(2)}) async-start(), calls=%async_computation.6 | async-start | bytes 1769472 | tf_op jit(solution)/shard_map/all_gather | solution.py:94
  44.2 5.3 %copy-start.4 = (bf16[128,2048]{1,0:T(8,128)(2,1)}, bf16[128,2048]{1,0:T(8,128)(2,1)S(1)}, u32[]{:S(2)}) copy-start(bf16[128,2048]{1,0:T(8,128)(2,1)S(1)} %gather_fusion.1) | copy-start | bytes 1572868
  50.4 3.5 %copy-start.6 = (bf16[128,2048]{1,0:T(8,128)(2,1)}, bf16[128,2048]{1,0:T(8,128)(2,1)S(1)}, u32[]{:S(2)}) copy-start(bf16[128,2048]{1,0:T(8,128)(2,1)S(1)} %gather_fusion.3) | copy-start | bytes 1572868
  53.9 3.2 %copy-start.3 = (f32[128,768]{1,0:T(8,128)}, f32[128,768]{1,0:T(8,128)S(1)}, u32[]{:S(2)}) copy-start(f32[128,768]{1,0:T(8,128)S(1)} %get-tuple-element.448) | copy-start | bytes 1179652
  72.0 8.9 %copy-start.2 = (bf16[128,2048]{1,0:T(8,128)(2,1)S(1)}, bf16[128,2048]{1,0:T(8,128)(2,1)}, u32[]{:S(2)}) copy-start(bf16[128,2048]{1,0:T(8,128)(2,1)} %get-tuple-element.307) | copy-start | bytes 1572868
  72.0 66.1 %all-gather.6.cloned.1.call-start = ((), (), s32[]{:S(2)}) async-start(), calls=%async_computation.7 | async-start | bytes 1769472 | tf_op jit(solution)/shard_map/all_gather | solution.py:95
  72.8 16.7 %copy-start.5 = (bf16[128,2048]{1,0:T(8,128)(2,1)S(1)}, bf16[128,2048]{1,0:T(8,128)(2,1)}, u32[]{:S(2)}) copy-start(bf16[128,2048]{1,0:T(8,128)(2,1)} %copy-done.4) | copy-start | bytes 1572868
  72.8 16.7 %copy-start.7 = (bf16[128,2048]{1,0:T(8,128)(2,1)S(1)}, bf16[128,2048]{1,0:T(8,128)(2,1)}, u32[]{:S(2)}) copy-start(bf16[128,2048]{1,0:T(8,128)(2,1)} %copy-done.6) | copy-start | bytes 1572868
  76.0 10.1 %all-to-all-start.2 = ((bf16[4,24,2048]{2,1,0:T(8,128)(2,1)}), bf16[4,24,2048]{2,1,0:T(8,128)(2,1)S(1)}, u32[]{:S(2)}, u32[]{:S(2)}) async-start(bf16[4,24,2048]{2,1,0:T(8,128)(2,1)} %bitcast.11), calls=%async_computation.2 | async-start | bytes 786432 | tf_op jit(solution)/shard_map/all_to_all | solution.py:152
  80.2 75.5 %all-gather.8.cloned.1.call-start = ((), (), s32[]{:S(2)}) async-start(), calls=%async_computation.8 | async-start | bytes 1769472 | tf_op jit(solution)/shard_map/all_gather | solution.py:96
  82.5 18.0 %copy-start.10 = (s32[1024,1]{0,1:T(1,128)S(1)}, s32[1024,1]{0,1:T(1,128)}, u32[]{:S(2)}) copy-start(s32[1024,1]{0,1:T(1,128)} %get-tuple-element.348) | copy-start | bytes 12292
  86.0 9.3 %all-to-all-start.3 = ((bf16[4,24,2048]{2,1,0:T(8,128)(2,1)}), bf16[4,24,2048]{2,1,0:T(8,128)(2,1)S(1)}, u32[]{:S(2)}, u32[]{:S(2)}) async-start(bf16[4,24,2048]{2,1,0:T(8,128)(2,1)} %bitcast.15), calls=%async_computation.3 | async-start | bytes 786432 | tf_op jit(solution)/shard_map/all_to_all | solution.py:159
  95.3 26.5 %all-to-all-start.4 = ((bf16[128,8,256]{2,0,1:T(8,128)(2,1)}), bf16[128,8,256]{2,0,1:T(8,128)(2,1)S(1)}, u32[]{:S(2)}, u32[]{:S(2)}) async-start(bf16[128,8,256]{2,0,1:T(8,128)(2,1)} %get-tuple-element.350), calls=%async_computation.4 | async-start | bytes 1048576 | tf_op jit(solution)/shard_map/all_to_all | solution.py:89
  112.5 13.1 %copy-start.9 = (f32[128,8]{1,0:T(8,128)S(1)}, f32[128,8]{1,0:T(8,128)}, u32[]{:S(2)}) copy-start(f32[128,8]{1,0:T(8,128)} %copy-done.8) | copy-start | bytes 12292
  121.8 18.8 %all-to-all-start.5 = ((bf16[128,8,256]{2,0,1:T(8,128)(2,1)}), bf16[128,8,256]{2,0,1:T(8,128)(2,1)S(1)}, u32[]{:S(2)}, u32[]{:S(2)}) async-start(bf16[128,8,256]{2,0,1:T(8,128)(2,1)} %get-tuple-element.351), calls=%async_computation.5 | async-start | bytes 1048576 | tf_op jit(solution)/shard_map/all_to_all | solution.py:90
Sparse Core Ops, SparseCore 0:
  72.1 26.9 all-gather.3
  100.8 28.8 all-gather.5
  131.3 24.2 all-gather.7
where the time goes:
time: 166 us; the launch traced here: 165 us
  local copies, waits for them, and re-layouts  43.1 us (26%)
  waiting for transfers between devices  30.8 us (19%)
  other arithmetic  25.9 us (16%)
  starting transfers between devices  25.4 us (15%)
  matrix products  25.4 us (15%)
  between operations  14.8 us (9%)
    all_gather x1, waiting for transfers between devices, run_expert(): hidden_piece = lax.all_gather(hidden_all, 'dp', axis=0, tiled=True)  15.1 us
    reduce_sum x1, other arithmetic, per_device(): grad_tokens = jnp.sum(took_part, axis=1).astype(jnp.bfloat16)  10.4 us
    gather x1, local copies, waits for them, and re-layouts, per_device(): back_out.reshape(slot_total, model_width)[safe_slot].astype(jnp.float32)  6.03 us
    gather x1, local copies, waits for them, and re-layouts, per_device(): back_part.reshape(slot_total, model_width)[safe_slot].astype(jnp.float32)  6.01 us
    all_to_all x1, waiting for transfers between devices, run_expert(): lax.all_to_all(split_x, 'dp', split_axis=1, concat_axis=0, tiled=True)  5.3 us
    all_to_all x1, starting transfers between devices, per_device(): lax.all_to_all(send_x.reshape(held_count, CAP, model_width), 'expert', sp...  5.19 us
    all_to_all x1, starting transfers between devices, run_expert(): lax.all_to_all(split_x, 'dp', split_axis=1, concat_axis=0, tiled=True)  4.88 us
    gather x2, local copies, waits for them, and re-layouts, run_expert(): return (out_all[placement], part_all[placement], summed)  4.73 us
  transfers between devices with their start and end apart: 9, of which 6 were waited for; matrix products, arithmetic and copies ran while one was open for 32% of the time, Pallas kernels for 0%

commit v1 on v0

--- a/solution.py
+++ b/solution.py
@@ -93,7 +93,9 @@
     recv_dy = recv_dy.reshape(groups * padded_rows, width_part)
     gate_piece = lax.all_gather(gate_all, "dp", axis=0, tiled=True)
     up_piece = lax.all_gather(up_all, "dp", axis=0, tiled=True)
-    hidden_piece = lax.all_gather(hidden_all, "dp", axis=0, tiled=True)
+    hidden_piece = jnp.concatenate(
+        lax.all_to_all(jnp.stack([hidden_all] * lax.axis_size("dp")), "dp", 0, 0), axis=0
+    )
     gate_term = lax.dot_general(
         recv_x, gate_piece, contract_first, preferred_element_type=jnp.float32
     )

time: 166 us -> 206 us (1.24)
  blocking collectives: 0 us -> 24.3 us
  waiting for transfers between devices: 30.8 us -> 46 us
    all_to_all x1, waiting for transfers between devices: 0.49 us -> 33.4 us  [run_expert(): lax.all_to_all(jnp.stack([hidden_all] * lax.axis_size('dp')), 'dp', 0, 0)]
    all_to_all x0 -> x1, blocking collectives: none -> 24.3 us  [run_expert(): lax.all_to_all(split_dy, 'dp', split_axis=1, concat_axis=0, tiled=True)]
    all_gather x1 -> x0, waiting for transfers between devices: 15.1 us -> none  [run_expert(): hidden_piece = lax.all_gather(hidden_all, 'dp', axis=0, tiled=True)]
    all_to_all x1, waiting for transfers between devices: 5.3 us -> 2.58 us  [run_expert(): lax.all_to_all(split_x, 'dp', split_axis=1, concat_axis=0, tiled=True)]
    another operation x5 -> x6, local copies, waits for them, and re-layouts: 3.78 us -> 5.03 us
  transfers between devices with their start and end apart: 9 -> 8, of which waited for: 6 -> 5; matrix products, arithmetic and copies ran while one was open for 32% -> 25% of each run, Pallas kernels for 0% -> 0%
where the time goes in v1:
time: 206 us; the launch traced here: 205 us
  waiting for transfers between devices  46 us (22%)
  local copies, waits for them, and re-layouts  44.4 us (22%)
  matrix products  25.3 us (12%)
  other arithmetic  25.2 us (12%)
  starting transfers between devices  24.9 us (12%)
  blocking collectives  24.3 us (12%)
  between operations  15.1 us (7%)
    all_to_all x1, waiting for transfers between devices, run_expert(): lax.all_to_all(jnp.stack([hidden_all] * lax.axis_size('dp')), 'dp', 0, 0)  33.4 us
    all_to_all x1, blocking collectives, run_expert(): lax.all_to_all(split_dy, 'dp', split_axis=1, concat_axis=0, tiled=True)  24.3 us
    reduce_sum x1, other arithmetic, per_device(): grad_tokens = jnp.sum(took_part, axis=1).astype(jnp.bfloat16)  10.4 us
    gather x1, local copies, waits for them, and re-layouts, per_device(): back_out.reshape(slot_total, model_width)[safe_slot].astype(jnp.float32)  6.03 us
    gather x1, local copies, waits for them, and re-layouts, per_device(): back_part.reshape(slot_total, model_width)[safe_slot].astype(jnp.float32)  6.01 us
    all_to_all x1, starting transfers between devices, per_device(): lax.all_to_all(send_x.reshape(held_count, CAP, model_width), 'expert', sp...  5.19 us
    gather x2, local copies, waits for them, and re-layouts, run_expert(): return (out_all[placement], part_all[placement], summed)  4.76 us
    all_to_all x1, waiting for transfers between devices, per_device(): lax.all_to_all(part_rows.reshape(held_count, CAP, model_width), 'expert',...  4.67 us
  transfers between devices with their start and end apart: 8, of which 5 were waited for; matrix products, arithmetic and copies ran while one was open for 25% of the time, Pallas kernels for 0%

profile of v1, /device:TPU:0, one launch (start us, length us, event | category | flops | bytes accessed | tf_op | source)
XLA Modules:
  0.0 205.2 jit_solution(18073316370430640707)
XLA Ops:
  11.8 4.3 %scatter_custom_fusion.1 = s32[96]{0:T(128)S(1)} fusion(s32[1024]{0:T(1024)S(1)} %bitcast.108, s32[1024]{0:T(1024)S(1)} %add_select_fusion, s32[]{:T(128)} %copy.53), kind=kCustom, calls=%fused_computation.100 | custom fusion | bytes 388 | tf_op jit(solution)/shard_map/scatter | solution.py:124
  16.1 4.3 %scatter_custom_fusion = pred[96]{0:T(512)(128)(4,1)S(1)} fusion(s32[1024]{0:T(1024)S(1)} %bitcast.109, pred[1024]{0:T(1024)(128)(4,1)S(1)} %broadcast.261, pred[]{:T(512)} %constant.84.clone.1), kind=kCustom, calls=%fused_computation.92 | custom fusion | bytes 97 | tf_op jit(solution)/shard_map/scatter | solution.py:130
  22.2 5.2 %all-to-all-start = ((bf16[4,24,2048]{2,1,0:T(8,128)(2,1)}), bf16[4,24,2048]{2,1,0:T(8,128)(2,1)S(1)}, u32[]{:S(2)}, u32[]{:S(2)}) async-start(bf16[4,24,2048]{2,1,0:T(8,128)(2,1)} %broadcast_select_fusion.1), calls=%async_computation | async-start | bytes 786432 | tf_op jit(solution)/shard_map/all_to_all | solution.py:134
  28.5 4.3 %scatter_custom_fusion.3 = f32[96]{0:T(128)S(1)} fusion(s32[1024]{0:T(1024)S(1)} %bitcast.110, f32[1024]{0:T(1024)S(1)} %reshape.416, f32[]{:T(128)} %constant.94.clone.1), kind=kCustom, calls=%fused_computation.95 | custom fusion | bytes 388 | tf_op jit(solution)/shard_map/scatter | solution.py:128
  34.0 3.9 %all-to-all-start.1 = ((bf16[4,24,2048]{2,1,0:T(8,128)(2,1)}), bf16[4,24,2048]{2,1,0:T(8,128)(2,1)S(1)}, u32[]{:S(2)}, u32[]{:S(2)}) async-start(bf16[4,24,2048]{2,1,0:T(8,128)(2,1)} %fusion.18), calls=%async_computation.1 | async-start | bytes 786432 | tf_op jit(solution)/shard_map/all_to_all | solution.py:141
  43.6 2.7 %negate_exponential_fusion = (f32[128,768]{1,0:T(8,128)S(1)}, f32[128,768]{1,0:T(8,128)S(1)}) fusion(bf16[2048,3,768]{2,0,1:T(8,128)(2,1)} %bitcast.111, bf16[128,2048]{1,0:T(8,128)(2,1)S(1)} %gather_fusion.1, pred[128]{0:T(512)(128)(4,1)S(1)} %iota_compare_fusion.2), kind=kOutput, calls=%fused_computation.56 | convolution fusion | flops 403013632 | bytes 4456576 | tf_op jit(solution)/shard_map/while/body/dot_general | solution.py:15
  49.8 3.5 %fusion.46 = (f32[128,768]{1,0:T(8,128)S(1)}, f32[128,768]{1,0:T(8,128)}) fusion(f32[128,768]{1,0:T(8,128)S(1)} %fusion.9, bf16[2048,3,768]{2,0,1:T(8,128)(2,1)} %bitcast.113, bf16[128,2048]{1,0:T(8,128)(2,1)S(1)} %gather_fusion.3, pred[128]{0:T(512)(128)(4,1)S(1)} %iota_compare_fusion.2), kind=kOutput, calls=%fused_computation.108 | convolution fusion | flops 403013632 | bytes 4849792 | tf_op jit(solution)/shard_map/while/body/dot_general | solution.py:23
  53.3 3.2 %fusion.14 = bf16[128,2048]{1,0:T(8,128)(2,1)S(1)} fusion(bf16[2048,3,768]{2,0,1:T(8,128)(2,1)} %bitcast.114, f32[128,768]{1,0:T(8,128)S(1)} %fusion.9, f32[128,768]{1,0:T(8,128)S(1)} %get-tuple-element.446), kind=kOutput, calls=%fused_computation.36 | convolution fusion | flops 403505152 | bytes 4456448 | tf_op jit(solution)/shard_map/while/body/dot_general | solution.py:20
  56.5 4.0 %fusion.6 = f32[128,2048]{1,0:T(8,128)} fusion(bf16[2048,3,768]{2,0,1:T(8,128)(2,1)} %bitcast.115, f32[128,768]{1,0:T(8,128)S(1)} %get-tuple-element.446, f32[128,768]{1,0:T(8,128)S(1)} %get-tuple-element.448), kind=kOutput, calls=%fused_computation.28 | convolution fusion | flops 403537920 | bytes 4980736 | tf_op jit(solution)/shard_map/while/body/dot_general | solution.py:29
  60.5 3.4 %fusion.13 = bf16[128,2048]{1,0:T(8,128)(2,1)S(1)} fusion(f32[128,2048]{1,0:T(8,128)} %fusion.6, bf16[2048,3,768]{2,0,1:T(8,128)(2,1)} %bitcast.116, f32[128,768]{1,0:T(8,128)} %get-tuple-element.449, f32[128,768]{1,0:T(8,128)S(1)} %get-tuple-element.446), kind=kOutput, calls=%fused_computation.35 | convolution fusion | flops 403767296 | bytes 5505024 | tf_op jit(solution)/shard_map/while/body/dot_general | solution.py:30
  67.7 3.6 %while.24 = (s32[]{:T(128)}, bf16[128,2048]{1,0:T(8,128)(2,1)}, bf16[128,2048]{1,0:T(8,128)(2,1)}, bf16[128,768]{1,0:T(8,128)(2,1)}, bf16[128,768]{1,0:T(8,128)(...) while((s32[]{:T(128)}, bf16[128,2048]{1,0:T(8,128)(2,1)}, ...), condition=%wide.region_12.13_spmd, body=%wide.region_11.12_spmd.sunk | while | flops 1277954 | bytes 4653197 | solution.py:80
  71.4 3.2 %gather_fusion.4 = bf16[96,2048]{1,0:T(8,128)(2,1)} fusion(bf16[128,2048]{1,0:T(8,128)(2,1)} %get-tuple-element.306, s32[1024]{0:T(1024)S(1)} %pad_clamp_fusion), kind=kCustom, calls=%fused_computation.4 | custom fusion | bytes 786816 | tf_op jit(solution)/shard_map/gather | solution.py:108
  74.6 4.3 %all-to-all-start.2 = ((bf16[4,24,2048]{2,1,0:T(8,128)(2,1)}), bf16[4,24,2048]{2,1,0:T(8,128)(2,1)S(1)}, u32[]{:S(2)}, u32[]{:S(2)}) async-start(bf16[4,24,2048]{2,1,0:T(8,128)(2,1)} %bitcast.101), calls=%async_computation.2 | async-start | bytes 786432 | tf_op jit(solution)/shard_map/all_to_all | solution.py:154
  81.2 3.6 %all-to-all-done.2 = bf16[4,24,2048]{2,1,0:T(8,128)(2,1)S(1)} async-done(((bf16[4,24,2048]{2,1,0:T(8,128)(2,1)}), bf16[4,24,2048]{2,1,0:T(8,128)(2,1)S(1)}, u32[]{:S(2)}, u32[]{:S(2)}) %all-to-all-start.2) | async-done | bytes 393248 | tf_op jit(solution)/shard_map/all_to_all | solution.py:154
  84.8 3.5 %all-to-all-start.3 = ((bf16[4,24,2048]{2,1,0:T(8,128)(2,1)}), bf16[4,24,2048]{2,1,0:T(8,128)(2,1)S(1)}, u32[]{:S(2)}, u32[]{:S(2)}) async-start(bf16[4,24,2048]{2,1,0:T(8,128)(2,1)} %bitcast.102), calls=%async_computation.3 | async-start | bytes 786432 | tf_op jit(solution)/shard_map/all_to_all | solution.py:161
  89.4 4.7 %all-to-all-done.3 = bf16[4,24,2048]{2,1,0:T(8,128)(2,1)S(1)} async-done(((bf16[4,24,2048]{2,1,0:T(8,128)(2,1)}), bf16[4,24,2048]{2,1,0:T(8,128)(2,1)S(1)}, u32[]{:S(2)}, u32[]{:S(2)}) %all-to-all-start.3) | async-done | bytes 393248 | tf_op jit(solution)/shard_map/all_to_all | solution.py:161
  94.1 24.3 %all_to_all.55 = bf16[128,8,256]{2,0,1:T(8,128)(2,1)} all-to-all(bf16[128,8,256]{2,0,1:T(8,128)(2,1)} %get-tuple-element.351), channel_id=1, replica_groups=mesh['dp'=8,'expert'=4] {'dp'}, dimensions={1} | all-to-all | bytes 1048576 | tf_op jit(solution)/shard_map/all_to_all | solution.py:90
  119.6 4.3 %all-to-all-start.6 = ((bf16[8,128,768]{2,1,0:T(8,128)(2,1)}), bf16[8,128,768]{2,1,0:T(8,128)(2,1)}, u32[]{:S(2)}, u32[]{:S(2)}) async-start(bf16[8,128,768]{2,1,0:T(8,128)(2,1)} %stack.12), calls=%async_computation.6 | async-start | bytes 3145728 | tf_op jit(solution)/shard_map/all_to_all | solution.py:97
  124.9 6.0 %gather_fusion.5 = bf16[1024,2048]{1,0:T(8,128)(2,1)} fusion(bf16[96,2048]{1,0:T(8,128)(2,1)S(1)} %bitcast.92, s32[1024]{0:T(1024)S(1)} %broadcast_clamp_fusion), kind=kCustom, calls=%fused_computation.5 | custom fusion | bytes 8392704 | tf_op jit(solution)/shard_map/gather | solution.py:172
  130.9 6.0 %gather_fusion.7 = bf16[1024,2048]{1,0:T(8,128)(2,1)} fusion(bf16[96,2048]{1,0:T(8,128)(2,1)S(1)} %bitcast.93, s32[1024]{0:T(1024)S(1)} %broadcast_clamp_fusion), kind=kCustom, calls=%fused_computation.7 | custom fusion | bytes 8392704 | tf_op jit(solution)/shard_map/gather | solution.py:177
  136.9 3.2 %fusion.4 = f32[1024]{0:T(1024)S(1)} fusion(bf16[1024,2048]{1,0:T(8,128)(2,1)} %gather_fusion.5, f32[128,2048]{1,0:T(8,128)S(1)} %convert_element_type.142, pred[1024]{0:T(1024)(128)(4,1)S(1)} %broadcast_in_dim.103), kind=kLoop, calls=%fused_computation.22 | loop fusion | flops 8387584 | bytes 5248000 | tf_op jit(solution)/shard_map/reduce_sum | solution.py:181
  140.9 33.4 %all-to-all-done.6 = bf16[8,128,768]{2,1,0:T(8,128)(2,1)} async-done(((bf16[8,128,768]{2,1,0:T(8,128)(2,1)}), bf16[8,128,768]{2,1,0:T(8,128)(2,1)}, u32[]{:S(2)}, u32[]{:S(2)}) %all-to-all-start.6) | async-done | bytes 1572896 | tf_op jit(solution)/shard_map/all_to_all | solution.py:97
  174.4 3.7 %all-to-all-start.4 = ((bf16[128,8,256]{2,0,1:T(8,128)(2,1)}), bf16[128,8,256]{2,0,1:T(8,128)(2,1)S(1)}, u32[]{:S(2)}, u32[]{:S(2)}) async-start(bf16[128,8,256]{2,0,1:T(8,128)(2,1)} %get-tuple-element.350), calls=%async_computation.4 | async-start | bytes 1048576 | tf_op jit(solution)/shard_map/all_to_all | solution.py:89
  178.1 10.4 %fusion.5 = (bf16[128,2048]{1,0:T(8,128)(2,1)}, bf16[128,2048]{1,0:T(8,128)(2,1)}) fusion(bf16[1024,2048]{1,0:T(8,128)(2,1)} %gather_fusion.7, pred[128,8]{1,0:T(8,128)(4,1)S(1)} %copy.15, bf16[1024,2048]{1,0:T(8,128)(2,1)} %gather_fusion.5, f32[128,8]{1,0:T(8,128)S(1)} %copy.14), kind=kLoop, calls=%fused_computation.24 | loop fusion | flops 14155776 | bytes 9442304 | tf_op jit(solution)/shard_map/reduce_sum | solution.py:182
  (100 shorter events, 40.6 us)
Async XLA Ops:
  7.2 13.4 %copy-start = (bf16[128,2048]{1,0:T(8,128)(2,1)S(1)}, bf16[128,2048]{1,0:T(8,128)(2,1)}, u32[]{:S(2)}) copy-start(bf16[128,2048]{1,0:T(8,128)(2,1)} %param.7) | copy-start | bytes 1572868
  7.2 20.2 %copy-start.1 = (bf16[128,2048]{1,0:T(8,128)(2,1)S(1)}, bf16[128,2048]{1,0:T(8,128)(2,1)}, u32[]{:S(2)}) copy-start(bf16[128,2048]{1,0:T(8,128)(2,1)} %param.10) | copy-start | bytes 1572868
  20.5 7.7 %copy-start.10 = (f32[128,8]{0,1:T(8,128)S(1)}, f32[128,8]{0,1:T(8,128)}, u32[]{:S(2)}) copy-start(f32[128,8]{0,1:T(8,128)} %param.9) | copy-start | bytes 12292
  22.2 11.8 %all-to-all-start = ((bf16[4,24,2048]{2,1,0:T(8,128)(2,1)}), bf16[4,24,2048]{2,1,0:T(8,128)(2,1)S(1)}, u32[]{:S(2)}, u32[]{:S(2)}) async-start(bf16[4,24,2048]{2,1,0:T(8,128)(2,1)} %broadcast_select_fusion.1), calls=%async_computation | async-start | bytes 786432 | tf_op jit(solution)/shard_map/all_to_all | solution.py:134
  34.0 14.8 %all-to-all-start.1 = ((bf16[4,24,2048]{2,1,0:T(8,128)(2,1)}), bf16[4,24,2048]{2,1,0:T(8,128)(2,1)S(1)}, u32[]{:S(2)}, u32[]{:S(2)}) async-start(bf16[4,24,2048]{2,1,0:T(8,128)(2,1)} %fusion.18), calls=%async_computation.1 | async-start | bytes 786432 | tf_op jit(solution)/shard_map/all_to_all | solution.py:141
  43.6 5.3 %copy-start.4 = (bf16[128,2048]{1,0:T(8,128)(2,1)}, bf16[128,2048]{1,0:T(8,128)(2,1)S(1)}, u32[]{:S(2)}) copy-start(bf16[128,2048]{1,0:T(8,128)(2,1)S(1)} %gather_fusion.1) | copy-start | bytes 1572868
  49.8 3.5 %copy-start.6 = (bf16[128,2048]{1,0:T(8,128)(2,1)}, bf16[128,2048]{1,0:T(8,128)(2,1)S(1)}, u32[]{:S(2)}) copy-start(bf16[128,2048]{1,0:T(8,128)(2,1)S(1)} %gather_fusion.3) | copy-start | bytes 1572868
  53.3 3.2 %copy-start.3 = (f32[128,768]{1,0:T(8,128)}, f32[128,768]{1,0:T(8,128)S(1)}, u32[]{:S(2)}) copy-start(f32[128,768]{1,0:T(8,128)S(1)} %get-tuple-element.448) | copy-start | bytes 1179652
  71.4 8.2 %copy-start.2 = (bf16[128,2048]{1,0:T(8,128)(2,1)S(1)}, bf16[128,2048]{1,0:T(8,128)(2,1)}, u32[]{:S(2)}) copy-start(bf16[128,2048]{1,0:T(8,128)(2,1)} %get-tuple-element.307) | copy-start | bytes 1572868
  71.4 16.9 %copy-start.5 = (bf16[128,2048]{1,0:T(8,128)(2,1)S(1)}, bf16[128,2048]{1,0:T(8,128)(2,1)}, u32[]{:S(2)}) copy-start(bf16[128,2048]{1,0:T(8,128)(2,1)} %copy-done.4) | copy-start | bytes 1572868
  71.4 16.9 %copy-start.7 = (bf16[128,2048]{1,0:T(8,128)(2,1)S(1)}, bf16[128,2048]{1,0:T(8,128)(2,1)}, u32[]{:S(2)}) copy-start(bf16[128,2048]{1,0:T(8,128)(2,1)} %copy-done.6) | copy-start | bytes 1572868
  74.6 43.8 %copy-start.9 = (bf16[128,768]{1,0:T(8,128)(2,1)S(1)}, bf16[128,768]{1,0:T(8,128)(2,1)}, u32[]{:S(2)}) copy-start(bf16[128,768]{1,0:T(8,128)(2,1)} %get-tuple-element.310) | copy-start | bytes 589828
  74.6 10.2 %all-to-all-start.2 = ((bf16[4,24,2048]{2,1,0:T(8,128)(2,1)}), bf16[4,24,2048]{2,1,0:T(8,128)(2,1)S(1)}, u32[]{:S(2)}, u32[]{:S(2)}) async-start(bf16[4,24,2048]{2,1,0:T(8,128)(2,1)} %bitcast.101), calls=%async_computation.2 | async-start | bytes 786432 | tf_op jit(solution)/shard_map/all_to_all | solution.py:154
  78.9 114.2 %all-gather.3.cloned.1.call-start = ((), (), s32[]{:S(2)}) async-start(), calls=%async_computation.7 | async-start | bytes 1769472 | tf_op jit(solution)/shard_map/all_gather | solution.py:94
  84.8 9.3 %all-to-all-start.3 = ((bf16[4,24,2048]{2,1,0:T(8,128)(2,1)}), bf16[4,24,2048]{2,1,0:T(8,128)(2,1)S(1)}, u32[]{:S(2)}, u32[]{:S(2)}) async-start(bf16[4,24,2048]{2,1,0:T(8,128)(2,1)} %bitcast.102), calls=%async_computation.3 | async-start | bytes 786432 | tf_op jit(solution)/shard_map/all_to_all | solution.py:161
  119.6 54.7 %all-to-all-start.6 = ((bf16[8,128,768]{2,1,0:T(8,128)(2,1)}), bf16[8,128,768]{2,1,0:T(8,128)(2,1)}, u32[]{:S(2)}, u32[]{:S(2)}) async-start(bf16[8,128,768]{2,1,0:T(8,128)(2,1)} %stack.12), calls=%async_computation.6 | async-start | bytes 3145728 | tf_op jit(solution)/shard_map/all_to_all | solution.py:97
  123.9 71.2 %all-gather.5.cloned.1.call-start = ((), (), s32[]{:S(2)}) async-start(), calls=%async_computation.8 | async-start | bytes 1769472 | tf_op jit(solution)/shard_map/all_gather | solution.py:95
  174.4 18.8 %all-to-all-start.4 = ((bf16[128,8,256]{2,0,1:T(8,128)(2,1)}), bf16[128,8,256]{2,0,1:T(8,128)(2,1)S(1)}, u32[]{:S(2)}, u32[]{:S(2)}) async-start(bf16[128,8,256]{2,0,1:T(8,128)(2,1)} %get-tuple-element.350), calls=%async_computation.4 | async-start | bytes 1048576 | tf_op jit(solution)/shard_map/all_to_all | solution.py:89
  178.1 10.4 %copy-start.8 = (bf16[128,8,256]{2,0,1:T(8,128)(2,1)S(1)}, bf16[128,8,256]{2,0,1:T(8,128)(2,1)}, u32[]{:S(2)}) copy-start(bf16[128,8,256]{2,0,1:T(8,128)(2,1)} %all_to_all.55) | copy-start | bytes 1572868
Sparse Core Ops, SparseCore 0:
  81.3 31.5 all-gather.2
  126.4 44.4 all-gather.4
